TPU v7x, 1024 devices: a whole 4x4x32 slice. The times are simulated.
1024 devices in a mesh: blk: 32 (over z_lo, x), freq: 32 (over z_hi, y, core).
Axes of the slice: x: 4, y: 4, z: 32 (z_hi: 4, z_lo: 8; z = z_hi * 8 + z_lo), core: 2. Of those that a mesh axis runs over, the one named last changes fastest.
Arguments:
- shot_rows: bfloat16 [2, 32, 256, 4096], P(None, 'freq', None, 'blk'), may hold values from -6 to 6
- surface_op: bfloat16 [2, 32, 4096, 4096], P(None, 'freq', None, 'blk'), may hold values from -0.09375 to 0.09375
- aperture: int32 [32, 32, 32], P('freq', None, 'blk'), may hold values from 0 to 1, as said below
Outputs:
- traces: float32 [256, 16, 4096], P('freq', None, 'blk')
Inputs may be any that keep to these rules, and one draw needn't show every extreme that they name: aperture[f, b, b] is 1 for every f and b.
All inputs are finite; a program needn't handle non-finite values.
Results may differ from a plain program's by a relative error of at most 0.0003.
Values may be sent and summed in bfloat16 or wider, within the bound.
No kernel may reach another device: no remote copies, remote signals or barrier semaphores. Data moves between devices by JAX's collectives and lax.ppermute only.
A program may use at most 32 MiB of HBM per device.

v0:
```python
import math

import jax
import jax.numpy as jnp
from jax import lax
from jax.sharding import PartitionSpec as P

NT = 16
PERIOD = 4096
BINS = 2048


def phase_tables(slices, total):
    bins = 1 + slices * (BINS // total)
    times = jnp.arange(NT, dtype=jnp.int32)
    phase = bins[:, None] * times[None, :] % PERIOD
    theta = 2.0 * math.pi * phase.astype(jnp.float32) / PERIOD
    return (jnp.cos(theta), jnp.sin(theta))


def to_time(frequency_spectra, cosine_table, sine_table, total):
    upper_bound = lax.Precision.HIGHEST
    output_traces = jnp.einsum(
        "hd,hki->kdi", cosine_table, frequency_spectra[0], precision=upper_bound
    ) - jnp.einsum("hd,hki->kdi", sine_table, frequency_spectra[1], precision=upper_bound)
    return output_traces * (1.0 / math.sqrt(total))


def block_product(block_portion, receiver_rows):
    real_values = jnp.einsum(
        "wzx,wxu->wzu", block_portion[0], receiver_rows[0], preferred_element_type=jnp.float32
    ) - jnp.einsum(
        "wzx,wxu->wzu", block_portion[1], receiver_rows[1], preferred_element_type=jnp.float32
    )
    imaginary_values = jnp.einsum(
        "wzx,wxu->wzu", block_portion[0], receiver_rows[1], preferred_element_type=jnp.float32
    ) + jnp.einsum(
        "wzx,wxu->wzu", block_portion[1], receiver_rows[0], preferred_element_type=jnp.float32
    )
    return jnp.stack([real_values, imaginary_values])


def per_device(shot_rows, surface_op, aperture):
    width = surface_op.shape[3]
    local_freqs = shot_rows.shape[1]
    keep = jnp.repeat(aperture[:, :, 0], width, axis=1)
    masked_blocks = surface_op * keep[None, :, :, None].astype(jnp.bfloat16)
    frequency_spectra = block_product(
        lax.all_gather(shot_rows, "blk", axis=3, tiled=True), masked_blocks
    )
    total = local_freqs * lax.axis_size("freq")
    slices = lax.axis_index("freq") * local_freqs + jnp.arange(local_freqs, dtype=jnp.int32)
    cosine_table, sine_table = phase_tables(slices, total)
    return lax.psum_scatter(
        to_time(frequency_spectra, cosine_table, sine_table, total),
        "freq",
        scatter_dimension=0,
        tiled=True,
    )


def solution(mesh):
    return jax.shard_map(
        per_device,
        mesh=mesh,
        in_specs=(
            P(None, "freq", None, "blk"),
            P(None, "freq", None, "blk"),
            P("freq", None, "blk"),
        ),
        out_specs=P("freq", None, "blk"),
        check_vma=False,
    )
```

profile of v0, /device:TPU:6, one launch (start us, length us, event | category | flops | bytes accessed | tf_op | source)
XLA Modules:
  0.0 416.2 jit_solution(18234005717232519843)
XLA Ops:
  6.5 0.0 all-gather.2.cloned.1.call-start
  6.5 0.7 all-gather.2.cloned.1.call-update
  7.3 0.0 reduce-scatter.2.cloned.1.call-start
  7.3 0.1 fusion.11
  7.4 0.7 convert_bitcast_fusion
  8.0 0.1 broadcast_bitcast_fusion
  8.1 1.9 broadcast_multiply_fusion
  10.0 202.2 %all-gather.2.cloned.1.call-done = bf16[2,1,256,4096]{3,2,1,0:T(8,128)(2,1)} async-done(((bf16[2,1,256,128]{3,2,1,0:T(8,128)(2,1)}), bf16[2,1,256,4096]{3,2,1,0:T(8,128)(2,1)}) %all-gather.2.cloned.1.call-update) | async-done | bytes 4194320 | tf_op jit(solution)/shard_map/all_gather | solution.py:49
  212.2 2.4 fusion.1
  214.6 2.4 fusion.5
  217.1 0.1 copy.4
  217.2 2.4 fusion
  219.6 2.4 fusion.7
  222.1 0.1 copy.5
  222.2 1.8 multiply_bitcast_fusion
  223.9 0.0 reduce-scatter.2.cloned.1.call-update
  224.0 185.4 %reduce-scatter.2.cloned.1.call-done = f32[8,16,128]{2,1,0:T(8,128)} async-done(((f32[256,16,128]{2,1,0:T(8,128)}), f32[8,16,128]{2,1,0:T(8,128)}) %reduce-scatter.2.cloned.1.call-update) | async-done | bytes 65552 | tf_op jit(solution)/shard_map/reduce_scatter | solution.py:54
Async XLA Ops:
  6.5 205.7 %all-gather.2.cloned.1.call-start = ((), (), s32[]{:S(2)}) async-start(), calls=%async_computation.1 | async-start | bytes 4325376 | tf_op jit(solution)/shard_map/all_gather | solution.py:49
  7.3 402.1 %reduce-scatter.2.cloned.1.call-start = ((), (), s32[]{:S(2)}) async-start(), calls=%async_computation.2 | async-start | bytes 2162688 | tf_op jit(solution)/shard_map/reduce_scatter | solution.py:54
Sparse Core Ops, SparseCore 0:
  9.9 202.2 all-gather.1
  224.1 185.1 reduce-scatter.1
where the time goes:
time: 416 us
  waiting for transfers between devices  388 us (93%)
  between operations  13.5 us (3%)
  matrix products  9.77 us (2%)
  other arithmetic  4.41 us (1%)
    all_gather x1, waiting for transfers between devices, per_device(): lax.all_gather(shot_rows, 'blk', axis=3, tiled=True)  202 us
    reduce_scatter x1, waiting for transfers between devices, per_device(): lax.psum_scatter(to_time(frequency_spectra, cosine_table, sine_table, tot...  185 us
  transfers between devices with their start and end apart: 2, of which 2 were waited for; matrix products, arithmetic and copies ran while one was open for 1% of the time, Pallas kernels for 0%

commit v1 on v0

v1 whole, which is shorter than its diff:
```python
import math

import jax
import jax.numpy as jnp
import numpy as np
from jax import lax
from jax.sharding import Mesh, PartitionSpec as P

NT = 16
PERIOD = 4096
BINS = 2048
ZL, NX, ZH, NY, NC = 8, 4, 4, 4, 2
BLK = ("zl", "x")
FREQ = ("zh", "y", "c")


def transform_matrix(total):
    bins = 1 + np.arange(total) * (BINS // total)
    phase = bins[:, None] * np.arange(NT)[None, :] % PERIOD
    theta = (2.0 * math.pi * phase.astype(np.float32) / PERIOD).astype(np.float32)
    scale = 1.0 / math.sqrt(total)
    return np.stack([np.cos(theta) * scale, -np.sin(theta) * scale]).astype(np.float32)


def shift(value, step):
    return lax.ppermute(value, "x", [(i, (i + step) % NX) for i in range(NX)])


def per_device(shot_rows, surface_op, aperture):
    x = lax.axis_index("x")
    width = surface_op.shape[3]
    shots = shot_rows.shape[2]
    total = ZH * NY * NC

    rows = surface_op.reshape(2, ZL, NX, width, width)
    keep = aperture.reshape(ZL, NX).astype(jnp.bfloat16)

    def quarter(owner):
        part = lax.dynamic_index_in_dim(rows, owner, 2, keepdims=False)
        mask = lax.dynamic_index_in_dim(keep, owner, 1, keepdims=False)
        return part * mask[None, :, None, None]

    ops = [quarter(x)] + [shift(quarter((x + d) % NX), d) for d in (1, 3, 2)]
    own = shot_rows.reshape(2, shots, width)
    copies = jnp.broadcast_to(own[None], (ZL,) + own.shape)
    gathered = lax.all_to_all(copies, "zl", 0, 0, tiled=True)

    def product(op):
        wide = jnp.einsum("zpsk,qzkr->pqsr", gathered, op, preferred_element_type=jnp.float32)
        return jnp.stack([wide[0, 0] - wide[1, 1], wide[0, 1] + wide[1, 0]])

    spectra = product(ops[0])
    for d, op in zip((1, 3, 2), ops[1:]):
        spectra = spectra + shift(product(op), -d)

    mine = lax.all_to_all(
        spectra.reshape(2, total, shots // total, width), FREQ, 1, 1, tiled=True
    )
    return jnp.einsum(
        "pft,pfsr->str",
        jnp.asarray(transform_matrix(total)),
        mine,
        precision=lax.Precision.HIGHEST,
    )


def solution(mesh):
    fine = Mesh(
        mesh.devices.reshape(ZL, NX, ZH, NY, NC), BLK + FREQ
    )
    return jax.shard_map(
        per_device,
        mesh=fine,
        in_specs=(
            P(None, FREQ, None, BLK),
            P(None, FREQ, None, BLK),
            P(FREQ, None, BLK),
        ),
        out_specs=P(FREQ, None, BLK),
        check_vma=False,
    )
```

time: 416 us -> 155 us (0.37)
  the two profiles are of different devices: /device:TPU:6 before, /device:TPU:33 now
where the time goes in v1:
time: 155 us
  blocking collectives  70.4 us (45%)
  starting transfers between devices  34.8 us (22%)
  waiting for transfers between devices  34.1 us (22%)
  matrix products  8.04 us (5%)
  local copies, waits for them, and re-layouts  6.3 us (4%)
    all_to_all x1, blocking collectives, per_device(): lax.all_to_all(spectra.reshape(2, total, shots // total, width), FREQ, 1,...  70.4 us
    all_to_all x1, waiting for transfers between devices, per_device(): gathered = lax.all_to_all(copies, 'zl', 0, 0, tiled=True)  28.9 us
    ppermute x6, starting transfers between devices, shift(): return lax.ppermute(value, 'x', [(i, (i + step) % NX) for i in range(NX)])  22.7 us
    all_to_all x1, starting transfers between devices, per_device(): gathered = lax.all_to_all(copies, 'zl', 0, 0, tiled=True)  12.1 us
    dot_general x4, matrix products, product(): jnp.einsum('zpsk,qzkr->pqsr', gathered, op, preferred_element_type=jnp.fl...  7.09 us
    ppermute x6, waiting for transfers between devices, shift(): return lax.ppermute(value, 'x', [(i, (i + step) % NX) for i in range(NX)])  5.19 us
  transfers between devices with their start and end apart: 7, of which 3 were waited for; matrix products, arithmetic and copies ran while one was open for 7% of the time, Pallas kernels for 0%

profile of v1, /device:TPU:33, one launch (start us, length us, event | category | flops | bytes accessed | tf_op | source)
XLA Modules:
  0.0 154.5 jit_solution(5758104062905418129)
XLA Ops:
  0.0 0.0 copy-start.3
  0.0 0.0 copy-start
  0.0 2.3 %broadcast_in_dim.5 = bf16[8,2,256,128]{3,2,1,0:T(8,128)(2,1)} broadcast(bf16[2,256,128]{2,1,0:T(8,128)(2,1)} %bitcast.95), dimensions={1,2,3} | broadcast | bytes 1179648 | tf_op jit(solution)/shard_map/broadcast_in_dim | solution.py:45
  2.3 12.1 %all-to-all-start = ((bf16[8,2,256,128]{3,2,1,0:T(8,128)(2,1)}), bf16[8,2,256,128]{3,2,1,0:T(8,128)(2,1)}, u32[]{:S(2)}, u32[]{:S(2)}) async-start(bf16[8,2,256,128]{3,2,1,0:T(8,128)(2,1)} %broadcast_in_dim.5), calls=%async_computation | async-start | bytes 2097152 | tf_op jit(solution)/shard_map/all_to_all | solution.py:46
  14.4 0.0 copy-done.3
  14.4 0.1 convert_element_type.7
  14.5 0.0 copy-done
  14.5 1.2 constant_dynamic-slice_fusion.3
  15.7 0.0 copy-start.1
  15.7 1.4 copy.64
  17.0 0.2 dynamic-slice_reduce_fusion.3
  17.2 0.1 bitcast_multiply_fusion
  17.3 4.7 %collective-permute-start.4 = (bf16[2,8,128,128]{2,3,1,0:T(8,128)(2,1)S(1)}, bf16[2,8,128,128]{2,3,1,0:T(8,128)(2,1)}, u32[]{:S(2)}, u32[]{:S(2)}) collective-permute-start(bf16[2,8,128,128]{2,3,1,0:T(8,128)(2,1)S(1)} %bitcast_multiply_fusion), channel_id=1, source_target_pairs={{0,64},{32,96},{64,0},{96,32},{1,65},{33,97},{65,1},{97,33},{2,66}... | collective-permute-start | bytes 1572872 | tf_op jit(solution)/shard_map/ppermute | solution.py:26
  22.0 0.0 copy-done.1
  22.0 0.3 copy.62
  22.3 0.1 bitcast_multiply_fusion.2
  22.4 2.2 %collective-permute-start = (bf16[2,8,128,128]{2,3,1,0:T(8,128)(2,1)S(1)}, bf16[2,8,128,128]{2,3,1,0:T(8,128)(2,1)}, u32[]{:S(2)}, u32[]{:S(2)}) collective-permute-start(bf16[2,8,128,128]{2,3,1,0:T(8,128)(2,1)S(1)} %bitcast_multiply_fusion.2), channel_id=1, source_target_pairs={{0,32},{32,64},{64,96},{96,0},{1,33},{33,65},{65,97},{97,1},{2,34}... | collective-permute-start | bytes 1572872 | tf_op jit(solution)/shard_map/ppermute | solution.py:26
  24.6 0.3 copy.63
  24.9 0.1 bitcast_multiply_fusion.1
  25.0 4.3 %collective-permute-start.2 = (bf16[2,8,128,128]{2,3,1,0:T(8,128)(2,1)S(1)}, bf16[2,8,128,128]{2,3,1,0:T(8,128)(2,1)S(1)}, u32[]{:S(2)}, u32[]{:S(2)}) collective-permute-start(bf16[2,8,128,128]{2,3,1,0:T(8,128)(2,1)S(1)} %bitcast_multiply_fusion.1), channel_id=1, source_target_pairs={{0,96},{32,0},{64,32},{96,64},{1,97},{33,1},{65,33},{97,65},{2,98}... | collective-permute-start | bytes 1572872 | tf_op jit(solution)/shard_map/ppermute | solution.py:26
  29.3 0.3 copy.26
  29.6 1.2 collective-permute-done.4
  30.8 28.9 %all-to-all-done = bf16[8,2,256,128]{3,2,1,0:T(8,128)(2,1)} async-done(((bf16[8,2,256,128]{3,2,1,0:T(8,128)(2,1)}), bf16[8,2,256,128]{3,2,1,0:T(8,128)(2,1)}, u32[]{:S(2)}, u32[]{:S(2)}) %all-to-all-start) | async-done | bytes 1048608 | tf_op jit(solution)/shard_map/all_to_all | solution.py:46
  59.7 1.8 %convolution_bitcast_fusion = f32[2,2,256,128]{2,3,1,0:T(8,128)S(1)} fusion(bf16[2,8,128,128]{2,3,1,0:T(8,128)(2,1)} %collective-permute-done.4, bf16[8,2,256,128]{3,2,1,0:T(8,128)(2,1)} %all-to-all-done), kind=kOutput, calls=%fused_computation | convolution fusion | flops 268435456 | bytes 2097152 | tf_op jit(solution)/shard_map/zpsk,qzkr->pqsr/dot_general | solution.py:49
  61.6 6.3 %collective-permute-start.5 = (f32[2,256,128]{1,2,0:T(8,128)S(1)}, f32[2,256,128]{1,2,0:T(8,128)S(1)}, u32[]{:S(2)}, u32[]{:S(2)}) collective-permute-start(f32[2,256,128]{1,2,0:T(8,128)S(1)} %pad_maximum_fusion.2), channel_id=1, source_target_pairs={{0,64},{32,96},{64,0},{96,32},{1,65},{33,97},{65,1},{97,33},{2,66}... | collective-permute-start | bytes 786440 | tf_op jit(solution)/shard_map/ppermute | solution.py:26
  68.0 0.0 collective-permute-done
  68.0 1.9 %convolution_bitcast_fusion.2 = f32[2,2,256,128]{2,3,1,0:T(8,128)S(1)} fusion(bf16[2,8,128,128]{2,3,1,0:T(8,128)(2,1)} %collective-permute-done, bf16[8,2,256,128]{3,2,1,0:T(8,128)(2,1)} %all-to-all-done), kind=kOutput, calls=%fused_computation.2 | convolution fusion | flops 268435456 | bytes 2097152 | tf_op jit(solution)/shard_map/zpsk,qzkr->pqsr/dot_general | solution.py:49
  69.9 2.8 %collective-permute-start.1 = (f32[2,256,128]{1,2,0:T(8,128)S(1)}, f32[2,256,128]{1,2,0:T(8,128)S(1)}, u32[]{:S(2)}, u32[]{:S(2)}) collective-permute-start(f32[2,256,128]{1,2,0:T(8,128)S(1)} %pad_maximum_fusion), channel_id=1, source_target_pairs={{0,96},{32,0},{64,32},{96,64},{1,97},{33,1},{65,33},{97,65},{2,98}... | collective-permute-start | bytes 786440 | tf_op jit(solution)/shard_map/ppermute | solution.py:26
  72.7 0.0 collective-permute-done.2
  72.7 1.7 %convolution_bitcast_fusion.1 = f32[2,2,256,128]{2,3,1,0:T(8,128)S(1)} fusion(bf16[2,8,128,128]{2,3,1,0:T(8,128)(2,1)S(1)} %collective-permute-done.2, bf16[8,2,256,128]{3,2,1,0:T(8,128)(2,1)} %all-to-all-done), kind=kOutput, calls=%fused_computation.1 | convolution fusion | flops 268435456 | bytes 2097152 | tf_op jit(solution)/shard_map/zpsk,qzkr->pqsr/dot_general | solution.py:49
  74.5 2.5 %collective-permute-start.3 = (f32[2,256,128]{1,2,0:T(8,128)S(1)}, f32[2,256,128]{1,2,0:T(8,128)S(1)}, u32[]{:S(2)}, u32[]{:S(2)}) collective-permute-start(f32[2,256,128]{1,2,0:T(8,128)S(1)} %pad_maximum_fusion.1), channel_id=1, source_target_pairs={{0,32},{32,64},{64,96},{96,0},{1,33},{33,65},{65,97},{97,1},{2,34}... | collective-permute-start | bytes 786440 | tf_op jit(solution)/shard_map/ppermute | solution.py:26
  77.0 1.7 %convolution_bitcast_fusion.3 = f32[2,2,256,128]{2,3,0,1:T(8,128)S(1)} fusion(bf16[8,2,256,128]{3,2,1,0:T(8,128)(2,1)} %all-to-all-done, bf16[2,8,1,128,128]{3,4,1,0,2:T(8,128)(2,1)S(1)} %copy.26, bf16[8]{0:T(256)(128)(2,1)S(1)} %get-tuple-element.5), kind=kOutput, calls=%fused_computation.3 | convolution fusion | flops 269484032 | bytes 2097168 | tf_op jit(solution)/shard_map/zpsk,qzkr->pqsr/dot_general | solution.py:49
  78.7 0.0 copy-start.2
  78.7 0.0 collective-permute-done.5
  78.8 0.0 collective-permute-done.1
  78.8 4.0 %collective-permute-done.3 = f32[2,256,128]{1,2,0:T(8,128)S(1)} collective-permute-done((f32[2,256,128]{1,2,0:T(8,128)S(1)}, f32[2,256,128]{1,2,0:T(8,128)S(1)}, u32[]{:S(2)}, u32[]{:S(2)}) %collective-permute-start.3) | collective-permute-done | bytes 262176 | tf_op jit(solution)/shard_map/ppermute | solution.py:26
  82.8 0.1 fusion.10
  82.9 0.1 copy.39
  83.0 0.2 copy.40
  83.2 70.4 %all_to_all.10 = f32[2,32,8,128]{3,0,2,1:T(2,128)S(1)} all-to-all(f32[2,32,8,128]{3,0,2,1:T(2,128)S(1)} %copy.40), channel_id=1, replica_groups=mesh['zl'=8,'x'=4,'zh'=4,'y'=4,'c'=2] {'zh','y','c'}, dimensions={1} | all-to-all | bytes 524288 | tf_op jit(solution)/shard_map/all_to_all | solution.py:56
  153.6 0.0 copy-done.2
  153.6 1.0 convolution_bitcast_fusion.4
  (9 shorter events, 0.2 us)
Async XLA Ops:
  0.0 14.4 %copy-start.3 = (s32[1,32,1]{1,2,0:T(1,128)S(1)}, s32[1,32,1]{1,2,0:T(1,128)}, u32[]{:S(2)}) copy-start(s32[1,32,1]{1,2,0:T(1,128)} %param.6) | copy-start | bytes 388
  0.0 14.5 %copy-start = (bf16[2,1,4096,128]{3,2,1,0:T(8,128)(2,1)S(1)}, bf16[2,1,4096,128]{3,2,1,0:T(8,128)(2,1)}, u32[]{:S(2)}) copy-start(bf16[2,1,4096,128]{3,2,1,0:T(8,128)(2,1)} %param.5) | copy-start | bytes 6291460
  2.3 57.4 %all-to-all-start = ((bf16[8,2,256,128]{3,2,1,0:T(8,128)(2,1)}), bf16[8,2,256,128]{3,2,1,0:T(8,128)(2,1)}, u32[]{:S(2)}, u32[]{:S(2)}) async-start(bf16[8,2,256,128]{3,2,1,0:T(8,128)(2,1)} %broadcast_in_dim.5), calls=%async_computation | async-start | bytes 2097152 | tf_op jit(solution)/shard_map/all_to_all | solution.py:46
  15.7 6.4 %copy-start.1 = (bf16[2,8,1,128,128]{4,3,2,1,0:T(8,128)(2,1)S(1)}, bf16[2,8,1,128,128]{4,3,2,1,0:T(8,128)(2,1)}, u32[]{:S(2)}) copy-start(bf16[2,8,1,128,128]{4,3,2,1,0:T(8,128)(2,1)} %get-tuple-element.11) | copy-start | bytes 1572868
  17.3 13.4 %collective-permute-start.4 = (bf16[2,8,128,128]{2,3,1,0:T(8,128)(2,1)S(1)}, bf16[2,8,128,128]{2,3,1,0:T(8,128)(2,1)}, u32[]{:S(2)}, u32[]{:S(2)}) collective-permute-start(bf16[2,8,128,128]{2,3,1,0:T(8,128)(2,1)S(1)} %bitcast_multiply_fusion), channel_id=1, source_target_pairs={{0,64},{32,96},{64,0},{96,32},{1,65},{33,97},{65,1},{97,33},{2,66}... | collective-permute-start | bytes 1572872 | tf_op jit(solution)/shard_map/ppermute | solution.py:26
  22.4 45.5 %collective-permute-start = (bf16[2,8,128,128]{2,3,1,0:T(8,128)(2,1)S(1)}, bf16[2,8,128,128]{2,3,1,0:T(8,128)(2,1)}, u32[]{:S(2)}, u32[]{:S(2)}) collective-permute-start(bf16[2,8,128,128]{2,3,1,0:T(8,128)(2,1)S(1)} %bitcast_multiply_fusion.2), channel_id=1, source_target_pairs={{0,32},{32,64},{64,96},{96,0},{1,33},{33,65},{65,97},{97,1},{2,34}... | collective-permute-start | bytes 1572872 | tf_op jit(solution)/shard_map/ppermute | solution.py:26
  25.0 47.6 %collective-permute-start.2 = (bf16[2,8,128,128]{2,3,1,0:T(8,128)(2,1)S(1)}, bf16[2,8,128,128]{2,3,1,0:T(8,128)(2,1)S(1)}, u32[]{:S(2)}, u32[]{:S(2)}) collective-permute-start(bf16[2,8,128,128]{2,3,1,0:T(8,128)(2,1)S(1)} %bitcast_multiply_fusion.1), channel_id=1, source_target_pairs={{0,96},{32,0},{64,32},{96,64},{1,97},{33,1},{65,33},{97,65},{2,98}... | collective-permute-start | bytes 1572872 | tf_op jit(solution)/shard_map/ppermute | solution.py:26
  61.6 17.1 %collective-permute-start.5 = (f32[2,256,128]{1,2,0:T(8,128)S(1)}, f32[2,256,128]{1,2,0:T(8,128)S(1)}, u32[]{:S(2)}, u32[]{:S(2)}) collective-permute-start(f32[2,256,128]{1,2,0:T(8,128)S(1)} %pad_maximum_fusion.2), channel_id=1, source_target_pairs={{0,64},{32,96},{64,0},{96,32},{1,65},{33,97},{65,1},{97,33},{2,66}... | collective-permute-start | bytes 786440 | tf_op jit(solution)/shard_map/ppermute | solution.py:26
  69.9 8.9 %collective-permute-start.1 = (f32[2,256,128]{1,2,0:T(8,128)S(1)}, f32[2,256,128]{1,2,0:T(8,128)S(1)}, u32[]{:S(2)}, u32[]{:S(2)}) collective-permute-start(f32[2,256,128]{1,2,0:T(8,128)S(1)} %pad_maximum_fusion), channel_id=1, source_target_pairs={{0,96},{32,0},{64,32},{96,64},{1,97},{33,1},{65,33},{97,65},{2,98}... | collective-permute-start | bytes 786440 | tf_op jit(solution)/shard_map/ppermute | solution.py:26
  74.5 8.3 %collective-permute-start.3 = (f32[2,256,128]{1,2,0:T(8,128)S(1)}, f32[2,256,128]{1,2,0:T(8,128)S(1)}, u32[]{:S(2)}, u32[]{:S(2)}) collective-permute-start(f32[2,256,128]{1,2,0:T(8,128)S(1)} %pad_maximum_fusion.1), channel_id=1, source_target_pairs={{0,32},{32,64},{64,96},{96,0},{1,33},{33,65},{65,97},{97,1},{2,34}... | collective-permute-start | bytes 786440 | tf_op jit(solution)/shard_map/ppermute | solution.py:26
  78.7 74.9 %copy-start.2 = (f32[2,32,16,1]{1,2,0,3:T(8,128)S(1)}, f32[2,32,16,1]{1,2,0,3:T(8,128)}, u32[]{:S(2)}) copy-start(f32[2,32,16,1]{1,2,0,3:T(8,128)} %constant.58) | copy-start | bytes 12292

commit v2 on v1

v2 whole, which is shorter than its diff:
```python
import math

import jax
import jax.numpy as jnp
import numpy as np
from jax import lax
from jax.experimental import pallas as pl
from jax.experimental.pallas import tpu as pltpu
from jax.sharding import Mesh, PartitionSpec as P

NT = 16
PERIOD = 4096
BINS = 2048
ZQ, ZR, NX, ZH, NY, NC = 2, 4, 4, 4, 4, 2
BLK = ("zq", "zr", "x")
FREQ = ("zh", "y", "c")


def transform_matrix(total):
    bins = 1 + np.arange(total) * (BINS // total)
    phase = bins[:, None] * np.arange(NT)[None, :] % PERIOD
    theta = (2.0 * math.pi * phase.astype(np.float32) / PERIOD).astype(np.float32)
    scale = 1.0 / math.sqrt(total)
    return np.stack([np.cos(theta) * scale, -np.sin(theta) * scale]).astype(np.float32)


def product_kernel(place_ref, *refs):
    near_refs, (far_ref, op_ref, out_ref, rows_ref) = refs[:ZR], refs[ZR:]
    shots, width = far_ref.shape[2:]

    @pl.when(pl.program_id(0) == 0)
    def _():
        for part in range(2):
            for z in range(ZR):
                at = pl.ds(part * shots, shots)
                rows_ref[at, z * width : (z + 1) * width] = near_refs[z][part]
                rows_ref[at, (ZR + z) * width : (ZR + z + 1) * width] = far_ref[z, part]

    quad, mine = place_ref[0], place_ref[1]
    order = [quad * ZR + (mine ^ d) for d in range(ZR)]
    order += [(1 - quad) * ZR + z for z in range(ZR)]
    op = jnp.concatenate(
        [jnp.concatenate([op_ref[0, 0, z], op_ref[0, 1, z]], axis=1) for z in order], axis=0
    )
    wide = jnp.dot(rows_ref[...], op, preferred_element_type=jnp.float32)
    out_ref[0, 0] = wide[:shots, :width] - wide[shots:, width:]
    out_ref[0, 1] = wide[:shots, width:] + wide[shots:, :width]


def product(place, near, far, op):
    shots, width = far.shape[2:]
    depth = 2 * ZR * width
    return pl.pallas_call(
        product_kernel,
        out_shape=jax.ShapeDtypeStruct((NX, 2, shots, width), jnp.float32),
        grid_spec=pltpu.PrefetchScalarGridSpec(
            num_scalar_prefetch=1,
            grid=(NX,),
            in_specs=[pl.BlockSpec((2, shots, width), lambda i, q: (0, 0, 0))] * ZR
            + [
                pl.BlockSpec((ZR, 2, shots, width), lambda i, q: (0, 0, 0, 0)),
                pl.BlockSpec((1, 2, 2 * ZR, width, width), lambda i, q: (i, 0, 0, 0, 0)),
            ],
            out_specs=pl.BlockSpec((1, 2, shots, width), lambda i, q: (i, 0, 0, 0)),
            scratch_shapes=[pltpu.VMEM((2 * shots, depth), jnp.bfloat16)],
        ),
        compiler_params=pltpu.CompilerParams(vmem_limit_bytes=16 << 20),
        cost_estimate=pl.CostEstimate(
            flops=2 * NX * 2 * shots * depth * 2 * width,
            bytes_accessed=6 << 20,
            transcendentals=0,
        ),
    )(place, *near, far, op)


def per_device(shot_rows, surface_op, aperture):
    width = surface_op.shape[3]
    shots = shot_rows.shape[2]
    total = ZH * NY * NC
    place = jnp.stack([lax.axis_index("zq"), lax.axis_index("zr")]).astype(jnp.int32)

    own = shot_rows.reshape(2, shots, width)
    crossed = lax.ppermute(own, "zq", [(0, 1), (1, 0)])

    keep = aperture.reshape(ZQ * ZR, NX).astype(jnp.bfloat16)
    rows = surface_op.reshape(2, ZQ * ZR, NX, width, width) * keep[None, :, :, None, None]
    op = lax.all_to_all(jnp.transpose(rows, (2, 0, 1, 3, 4)), "x", 0, 0, tiled=True)

    near = [own] + [
        lax.ppermute(own, "zr", [(i, i ^ d) for i in range(ZR)]) for d in range(1, ZR)
    ]
    far = lax.all_gather(crossed, "zr", axis=0)

    parts = lax.all_to_all(product(place, near, far, op), "x", 0, 0, tiled=True)
    spectra = (parts[0] + parts[1]) + (parts[2] + parts[3])
    sent = jnp.transpose(spectra.reshape(2, total, shots // total, width), (1, 0, 2, 3))
    mine = lax.all_to_all(sent, FREQ, 0, 0, tiled=True)
    return jnp.einsum(
        "pft,fpsr->str",
        jnp.asarray(transform_matrix(total)),
        mine,
        precision=lax.Precision.HIGHEST,
    )


def solution(mesh):
    fine = Mesh(mesh.devices.reshape(ZQ, ZR, NX, ZH, NY, NC), BLK + FREQ)
    return jax.shard_map(
        per_device,
        mesh=fine,
        in_specs=(
            P(None, FREQ, None, BLK),
            P(None, FREQ, None, BLK),
            P(FREQ, None, BLK),
        ),
        out_specs=P(FREQ, None, BLK),
        check_vma=False,
    )
```

time: 155 us -> 139 us (0.90)
  blocking collectives: 70.4 us -> 107 us
  waiting for transfers between devices: 34.1 us -> 0.01 us
  starting transfers between devices: 34.8 us -> 22.9 us
  matrix products: 8.04 us -> 0.96 us
  local copies, waits for them, and re-layouts: 6.3 us -> 0.4 us
  other arithmetic: 0.61 us -> 3.94 us
  Pallas kernels: 0 us -> 2.67 us
    all_to_all x1, waiting for transfers between devices: 28.9 us -> 0.01 us  [per_device(): lax.all_to_all(jnp.transpose(rows, (2, 0, 1, 3, 4)), 'x', 0, 0, tiled=True)]
    all_to_all x1 -> x2, blocking collectives: 70.4 us -> 91 us  [the longest x1 74.5 us: per_device(): mine = lax.all_to_all(sent, FREQ, 0, 0, tiled=True)]
    all_gather x0 -> x1, blocking collectives: none -> 16.3 us  [per_device(): far = lax.all_gather(crossed, 'zr', axis=0)]
    all_to_all x1, starting transfers between devices: 12.1 us -> 4.14 us  [per_device(): lax.all_to_all(jnp.transpose(rows, (2, 0, 1, 3, 4)), 'x', 0, 0, tiled=True)]
    dot_general x5 -> x1, matrix products: 8.04 us -> 0.96 us  [per_device(): jnp.einsum('pft,fpsr->str', jnp.asarray(transform_matrix(total)), mine, p...]
    ppermute x6 -> x4, waiting for transfers between devices: 5.19 us -> 0.01 us  [the longest x3 0.01 us: per_device(): lax.ppermute(own, 'zr', [(i, i ^ d) for i in range(ZR)])]
    ppermute x6 -> x4, starting transfers between devices: 22.7 us -> 18.7 us  [the longest x3 9.91 us: per_device(): lax.ppermute(own, 'zr', [(i, i ^ d) for i in range(ZR)])]
    transpose x0 -> x1, other arithmetic: none -> 3.14 us  [per_device(): jnp.transpose(rows, (2, 0, 1, 3, 4))]
  transfers between devices with their start and end apart: 7 -> 5, of which waited for: 3 -> 0; matrix products, arithmetic and copies ran while one was open for 7% -> 0% of each run, Pallas kernels for 0% -> 0%
where the time goes in v2:
time: 139 us; the launch traced here: 138 us
  blocking collectives  107 us (77%)
  starting transfers between devices  22.9 us (16%)
  other arithmetic  3.94 us (3%)
  Pallas kernels  2.67 us (2%)
    all_to_all x1, blocking collectives, per_device(): mine = lax.all_to_all(sent, FREQ, 0, 0, tiled=True)  74.5 us
    all_to_all x1, blocking collectives, per_device(): parts = lax.all_to_all(product(place, near, far, op), 'x', 0, 0, tiled=True)  16.5 us
    all_gather x1, blocking collectives, per_device(): far = lax.all_gather(crossed, 'zr', axis=0)  16.3 us
    ppermute x3, starting transfers between devices, per_device(): lax.ppermute(own, 'zr', [(i, i ^ d) for i in range(ZR)])  9.91 us
    ppermute x1, starting transfers between devices, per_device(): crossed = lax.ppermute(own, 'zq', [(0, 1), (1, 0)])  8.81 us
    all_to_all x1, starting transfers between devices, per_device(): lax.all_to_all(jnp.transpose(rows, (2, 0, 1, 3, 4)), 'x', 0, 0, tiled=True)  4.14 us
    transpose x1, other arithmetic, per_device(): jnp.transpose(rows, (2, 0, 1, 3, 4))  3.14 us
  transfers between devices with their start and end apart: 5, of which 0 were waited for; matrix products, arithmetic and copies ran while one was open for 0% of the time, Pallas kernels for 0%

profile of v2, /device:TPU:33, one launch (start us, length us, event | category | flops | bytes accessed | tf_op | source)
XLA Modules:
  0.0 138.2 jit_solution(6506733206078685047)
XLA Ops:
  0.0 0.7 convert_reduce_fusion
  0.7 0.1 convert_element_type.11
  0.8 0.1 copy.10
  0.9 3.1 %fusion = bf16[4,2,8,128,128]{4,3,2,1,0:T(8,128)(2,1)} fusion(bf16[2,8,4,128,128]{4,3,2,1,0:T(8,128)(2,1)} %bitcast.25, bf16[8,4]{0,1:T(4,128)(2,1)S(1)} %copy.10), kind=kLoop, calls=%fused_computation.1 | loop fusion | flops 1048576 | bytes 4194368 | tf_op jit(solution)/shard_map/transpose | solution.py:87
  4.0 0.0 copy-start
  4.0 4.1 %all-to-all-start = ((bf16[4,2,8,128,128]{4,3,2,1,0:T(8,128)(2,1)}), bf16[4,2,8,128,128]{4,3,2,1,0:T(8,128)(2,1)S(1)}, u32[]{:S(2)}, u32[]{:S(2)}) async-start(bf16[4,2,8,128,128]{4,3,2,1,0:T(8,128)(2,1)} %fusion), calls=%async_computation | async-start | bytes 4194304 | tf_op jit(solution)/shard_map/all_to_all | solution.py:87
  8.1 0.0 copy-done
  8.2 8.8 %collective-permute-start.3 = (bf16[2,256,128]{2,1,0:T(8,128)(2,1)S(1)}, bf16[2,256,128]{2,1,0:T(8,128)(2,1)S(1)}, u32[]{:S(2)}, u32[]{:S(2)}) collective-permute-start(bf16[2,256,128]{2,1,0:T(8,128)(2,1)S(1)} %bitcast.20), channel_id=1, source_target_pairs={{0,512},{512,0},{1,513},{513,1},{2,514},{514,2},{3,515},{515,3},{4... | collective-permute-start | bytes 393224 | tf_op jit(solution)/shard_map/ppermute | solution.py:83
  17.0 3.5 %collective-permute-start.2 = (bf16[2,256,128]{2,1,0:T(8,128)(2,1)S(1)}, bf16[2,256,128]{2,1,0:T(8,128)(2,1)S(1)}, u32[]{:S(2)}, u32[]{:S(2)}) collective-permute-start(bf16[2,256,128]{2,1,0:T(8,128)(2,1)S(1)} %bitcast.21), channel_id=1, source_target_pairs={{0,384},{128,256},{256,128},{384,0},{1,385},{129,257},{257,129},{3... | collective-permute-start | bytes 393224 | tf_op jit(solution)/shard_map/ppermute | solution.py:90
  20.5 3.3 %collective-permute-start.1 = (bf16[2,256,128]{2,1,0:T(8,128)(2,1)S(1)}, bf16[2,256,128]{2,1,0:T(8,128)(2,1)S(1)}, u32[]{:S(2)}, u32[]{:S(2)}) collective-permute-start(bf16[2,256,128]{2,1,0:T(8,128)(2,1)S(1)} %bitcast.22), channel_id=1, source_target_pairs={{0,256},{128,384},{256,0},{384,128},{1,257},{129,385},{257,1},{385... | collective-permute-start | bytes 393224 | tf_op jit(solution)/shard_map/ppermute | solution.py:90
  23.8 3.1 %collective-permute-start = (bf16[2,256,128]{2,1,0:T(8,128)(2,1)S(1)}, bf16[2,256,128]{2,1,0:T(8,128)(2,1)S(1)}, u32[]{:S(2)}, u32[]{:S(2)}) collective-permute-start(bf16[2,256,128]{2,1,0:T(8,128)(2,1)S(1)} %bitcast.23), channel_id=1, source_target_pairs={{0,128},{128,0},{256,384},{384,256},{1,129},{129,1},{257,385},{385... | collective-permute-start | bytes 393224 | tf_op jit(solution)/shard_map/ppermute | solution.py:90
  26.9 0.1 pad_add_fusion.place_ref
  27.0 0.0 collective-permute-done.3
  27.0 16.3 %all-gather = bf16[8,256,128]{2,1,0:T(8,128)(2,1)S(1)} all-gather(bf16[2,256,128]{2,1,0:T(8,128)(2,1)S(1)} %collective-permute-done.3), channel_id=2, replica_groups=mesh['zq'=2,'zr'=4,'x'=4,'zh'=4,'y'=4,'c'=2] {'zr'}, dimensions={0}, use_global_device_ids=true | all-gather | bytes 655360 | tf_op jit(solution)/shard_map/all_gather | solution.py:92
  43.3 0.0 collective-permute-done.2.refs_3_
  43.3 0.0 collective-permute-done.1.refs_2_
  43.3 0.0 collective-permute-done.refs_1_
  43.3 0.0 all-to-all-done.refs_5_
  43.4 2.7 %shard_map.46 = f32[4,2,256,128]{3,2,1,0:T(8,128)S(1)} custom-call(s32[2]{0:T(128)S(1)} %pad_add_fusion.place_ref, bf16[2,256,128]{2,1,0:T(8,128)(2,1)S(1)} %bitcast.24, bf16[2,256,128]{2,1,0:T(8,128)(2,1)S(1)} %collective-permute-done.refs_1_, bf16[2,256,128]{2,1,0:T(8,128)(2,1)S(1)} %collective-permute-done.1.refs_2_, ...), custom_call_target="tpu_custom_call" | custom-call | flops 1073741824 | bytes 6291456 | tf_op jit(solution)/shard_map/pallas_call | solution.py:53
  46.0 0.0 copy-start.1
  46.0 16.5 %all_to_all.15 = f32[4,2,256,128]{3,2,1,0:T(8,128)S(1)} all-to-all(f32[4,2,256,128]{3,2,1,0:T(8,128)S(1)} %shard_map.46), channel_id=1, replica_groups=mesh['zq'=2,'zr'=4,'x'=4,'zh'=4,'y'=4,'c'=2] {'x'}, dimensions={0} | all-to-all | bytes 2097152 | tf_op jit(solution)/shard_map/all_to_all | solution.py:94
  62.5 0.1 fusion.2
  62.6 0.2 copy.21
  62.8 74.5 %all_to_all.16 = f32[32,2,8,128]{3,1,2,0:T(2,128)S(1)} all-to-all(f32[32,2,8,128]{3,1,2,0:T(2,128)S(1)} %bitcast.26), channel_id=1, replica_groups=mesh['zq'=2,'zr'=4,'x'=4,'zh'=4,'y'=4,'c'=2] {'zh','y','c'}, dimensions={0} | all-to-all | bytes 524288 | tf_op jit(solution)/shard_map/all_to_all | solution.py:97
  137.3 0.0 copy-done.1
  137.3 1.0 convolution_bitcast_fusion
Async XLA Ops:
  4.0 4.1 %copy-start = (bf16[2,1,256,128]{3,2,1,0:T(8,128)(2,1)S(1)}, bf16[2,1,256,128]{3,2,1,0:T(8,128)(2,1)}, u32[]{:S(2)}) copy-start(bf16[2,1,256,128]{3,2,1,0:T(8,128)(2,1)} %param.4) | copy-start | bytes 393220
  4.0 39.3 %all-to-all-start = ((bf16[4,2,8,128,128]{4,3,2,1,0:T(8,128)(2,1)}), bf16[4,2,8,128,128]{4,3,2,1,0:T(8,128)(2,1)S(1)}, u32[]{:S(2)}, u32[]{:S(2)}) async-start(bf16[4,2,8,128,128]{4,3,2,1,0:T(8,128)(2,1)} %fusion), calls=%async_computation | async-start | bytes 4194304 | tf_op jit(solution)/shard_map/all_to_all | solution.py:87
  8.2 18.8 %collective-permute-start.3 = (bf16[2,256,128]{2,1,0:T(8,128)(2,1)S(1)}, bf16[2,256,128]{2,1,0:T(8,128)(2,1)S(1)}, u32[]{:S(2)}, u32[]{:S(2)}) collective-permute-start(bf16[2,256,128]{2,1,0:T(8,128)(2,1)S(1)} %bitcast.20), channel_id=1, source_target_pairs={{0,512},{512,0},{1,513},{513,1},{2,514},{514,2},{3,515},{515,3},{4... | collective-permute-start | bytes 393224 | tf_op jit(solution)/shard_map/ppermute | solution.py:83
  17.0 26.4 %collective-permute-start.2 = (bf16[2,256,128]{2,1,0:T(8,128)(2,1)S(1)}, bf16[2,256,128]{2,1,0:T(8,128)(2,1)S(1)}, u32[]{:S(2)}, u32[]{:S(2)}) collective-permute-start(bf16[2,256,128]{2,1,0:T(8,128)(2,1)S(1)} %bitcast.21), channel_id=1, source_target_pairs={{0,384},{128,256},{256,128},{384,0},{1,385},{129,257},{257,129},{3... | collective-permute-start | bytes 393224 | tf_op jit(solution)/shard_map/ppermute | solution.py:90
  20.5 22.8 %collective-permute-start.1 = (bf16[2,256,128]{2,1,0:T(8,128)(2,1)S(1)}, bf16[2,256,128]{2,1,0:T(8,128)(2,1)S(1)}, u32[]{:S(2)}, u32[]{:S(2)}) collective-permute-start(bf16[2,256,128]{2,1,0:T(8,128)(2,1)S(1)} %bitcast.22), channel_id=1, source_target_pairs={{0,256},{128,384},{256,0},{384,128},{1,257},{129,385},{257,1},{385... | collective-permute-start | bytes 393224 | tf_op jit(solution)/shard_map/ppermute | solution.py:90
  23.8 19.5 %collective-permute-start = (bf16[2,256,128]{2,1,0:T(8,128)(2,1)S(1)}, bf16[2,256,128]{2,1,0:T(8,128)(2,1)S(1)}, u32[]{:S(2)}, u32[]{:S(2)}) collective-permute-start(bf16[2,256,128]{2,1,0:T(8,128)(2,1)S(1)} %bitcast.23), channel_id=1, source_target_pairs={{0,128},{128,0},{256,384},{384,256},{1,129},{129,1},{257,385},{385... | collective-permute-start | bytes 393224 | tf_op jit(solution)/shard_map/ppermute | solution.py:90
  46.0 91.2 %copy-start.1 = (f32[2,32,16,1]{1,2,0,3:T(8,128)S(1)}, f32[2,32,16,1]{1,2,0,3:T(8,128)}, u32[]{:S(2)}) copy-start(f32[2,32,16,1]{1,2,0,3:T(8,128)} %constant.18) | copy-start | bytes 12292

commit v3 on v2

--- a/solution.py
+++ b/solution.py
@@ -93,8 +93,20 @@
 
     parts = lax.all_to_all(product(place, near, far, op), "x", 0, 0, tiled=True)
     spectra = (parts[0] + parts[1]) + (parts[2] + parts[3])
+    peak = jnp.maximum(jnp.max(jnp.abs(spectra)), 2.0**-100)
+    level = jnp.floor(jnp.log2(peak))
     sent = jnp.transpose(spectra.reshape(2, total, shots // total, width), (1, 0, 2, 3))
-    mine = lax.all_to_all(sent, FREQ, 0, 0, tiled=True)
+    sent = (sent * jnp.exp2(13.0 - level)).astype(jnp.float16)
+    sent = jnp.concatenate(
+        [
+            sent.reshape(total, shots // total, 2, width),
+            jnp.full((total, 1, 2, width), level, jnp.float16),
+        ],
+        axis=1,
+    )
+    mine = lax.all_to_all(sent, FREQ, 0, 0, tiled=True).astype(jnp.float32)
+    values = mine[:, :-1].reshape(total, 2, shots // total, width)
+    mine = values * jnp.exp2(mine[:, -1, 0] - 13.0)[:, None, None, :]
     return jnp.einsum(
         "pft,fpsr->str",
         jnp.asarray(transform_matrix(total)),

time: 139 us -> 131 us (0.942)
  blocking collectives: 107 us -> 98.1 us
    all_to_all x1, blocking collectives: 74.5 us -> 65.3 us  [per_device(): mine = lax.all_to_all(sent, FREQ, 0, 0, tiled=True).astype(jnp.float32)]
where the time goes in v3:
time: 131 us
  blocking collectives  98.1 us (75%)
  starting transfers between devices  22.9 us (17%)
  other arithmetic  4.6 us (4%)
  Pallas kernels  2.67 us (2%)
    all_to_all x1, blocking collectives, per_device(): mine = lax.all_to_all(sent, FREQ, 0, 0, tiled=True).astype(jnp.float32)  65.3 us
    all_to_all x1, blocking collectives, per_device(): parts = lax.all_to_all(product(place, near, far, op), 'x', 0, 0, tiled=True)  16.5 us
    all_gather x1, blocking collectives, per_device(): far = lax.all_gather(crossed, 'zr', axis=0)  16.3 us
    ppermute x3, starting transfers between devices, per_device(): lax.ppermute(own, 'zr', [(i, i ^ d) for i in range(ZR)])  9.91 us
    ppermute x1, starting transfers between devices, per_device(): crossed = lax.ppermute(own, 'zq', [(0, 1), (1, 0)])  8.81 us
    all_to_all x1, starting transfers between devices, per_device(): lax.all_to_all(jnp.transpose(rows, (2, 0, 1, 3, 4)), 'x', 0, 0, tiled=True)  4.14 us
    transpose x1, other arithmetic, per_device(): jnp.transpose(rows, (2, 0, 1, 3, 4))  3.13 us
    pallas_call x1, Pallas kernels, product(): pl.pallas_call(product_kernel, out_shape=jax.ShapeDtypeStruct((NX, 2, sho...  2.67 us
  transfers between devices with their start and end apart: 5, of which 0 were waited for; matrix products, arithmetic and copies ran while one was open for 0% of the time, Pallas kernels for 0%

profile of v3, /device:TPU:33, one launch (start us, length us, event | category | flops | bytes accessed | tf_op | source)
XLA Modules:
  0.0 130.6 jit_solution(4062596421824624801)
XLA Ops:
  0.0 0.7 convert_reduce_fusion
  0.7 0.1 convert_element_type.26
  0.8 0.1 copy.10
  0.9 3.1 %fusion = bf16[4,2,8,128,128]{4,3,2,1,0:T(8,128)(2,1)} fusion(bf16[2,8,4,128,128]{4,3,2,1,0:T(8,128)(2,1)} %bitcast.33, bf16[8,4]{0,1:T(4,128)(2,1)S(1)} %copy.10), kind=kLoop, calls=%fused_computation.1 | loop fusion | flops 1048576 | bytes 4194368 | tf_op jit(solution)/shard_map/transpose | solution.py:87
  4.0 0.0 copy-start
  4.0 4.1 %all-to-all-start = ((bf16[4,2,8,128,128]{4,3,2,1,0:T(8,128)(2,1)}), bf16[4,2,8,128,128]{4,3,2,1,0:T(8,128)(2,1)S(1)}, u32[]{:S(2)}, u32[]{:S(2)}) async-start(bf16[4,2,8,128,128]{4,3,2,1,0:T(8,128)(2,1)} %fusion), calls=%async_computation | async-start | bytes 4194304 | tf_op jit(solution)/shard_map/all_to_all | solution.py:87
  8.1 0.0 copy-done
  8.1 8.8 %collective-permute-start.3 = (bf16[2,256,128]{2,1,0:T(8,128)(2,1)S(1)}, bf16[2,256,128]{2,1,0:T(8,128)(2,1)S(1)}, u32[]{:S(2)}, u32[]{:S(2)}) collective-permute-start(bf16[2,256,128]{2,1,0:T(8,128)(2,1)S(1)} %bitcast.28), channel_id=1, source_target_pairs={{0,512},{512,0},{1,513},{513,1},{2,514},{514,2},{3,515},{515,3},{4... | collective-permute-start | bytes 393224 | tf_op jit(solution)/shard_map/ppermute | solution.py:83
  17.0 3.5 %collective-permute-start.2 = (bf16[2,256,128]{2,1,0:T(8,128)(2,1)S(1)}, bf16[2,256,128]{2,1,0:T(8,128)(2,1)S(1)}, u32[]{:S(2)}, u32[]{:S(2)}) collective-permute-start(bf16[2,256,128]{2,1,0:T(8,128)(2,1)S(1)} %bitcast.29), channel_id=1, source_target_pairs={{0,384},{128,256},{256,128},{384,0},{1,385},{129,257},{257,129},{3... | collective-permute-start | bytes 393224 | tf_op jit(solution)/shard_map/ppermute | solution.py:90
  20.5 3.3 %collective-permute-start.1 = (bf16[2,256,128]{2,1,0:T(8,128)(2,1)S(1)}, bf16[2,256,128]{2,1,0:T(8,128)(2,1)S(1)}, u32[]{:S(2)}, u32[]{:S(2)}) collective-permute-start(bf16[2,256,128]{2,1,0:T(8,128)(2,1)S(1)} %bitcast.30), channel_id=1, source_target_pairs={{0,256},{128,384},{256,0},{384,128},{1,257},{129,385},{257,1},{385... | collective-permute-start | bytes 393224 | tf_op jit(solution)/shard_map/ppermute | solution.py:90
  23.8 3.1 %collective-permute-start = (bf16[2,256,128]{2,1,0:T(8,128)(2,1)S(1)}, bf16[2,256,128]{2,1,0:T(8,128)(2,1)S(1)}, u32[]{:S(2)}, u32[]{:S(2)}) collective-permute-start(bf16[2,256,128]{2,1,0:T(8,128)(2,1)S(1)} %bitcast.31), channel_id=1, source_target_pairs={{0,128},{128,0},{256,384},{384,256},{1,129},{129,1},{257,385},{385... | collective-permute-start | bytes 393224 | tf_op jit(solution)/shard_map/ppermute | solution.py:90
  26.9 0.1 pad_add_fusion.place_ref
  27.0 0.0 collective-permute-done.3
  27.0 16.3 %all-gather = bf16[8,256,128]{2,1,0:T(8,128)(2,1)S(1)} all-gather(bf16[2,256,128]{2,1,0:T(8,128)(2,1)S(1)} %collective-permute-done.3), channel_id=2, replica_groups=mesh['zq'=2,'zr'=4,'x'=4,'zh'=4,'y'=4,'c'=2] {'zr'}, dimensions={0}, use_global_device_ids=true | all-gather | bytes 655360 | tf_op jit(solution)/shard_map/all_gather | solution.py:92
  43.3 0.0 collective-permute-done.2.refs_3_
  43.3 0.0 collective-permute-done.1.refs_2_
  43.3 0.0 collective-permute-done.refs_1_
  43.3 0.0 all-to-all-done.refs_5_
  43.3 2.7 %shard_map.46 = f32[4,2,256,128]{3,2,1,0:T(8,128)S(1)} custom-call(s32[2]{0:T(128)S(1)} %pad_add_fusion.place_ref, bf16[2,256,128]{2,1,0:T(8,128)(2,1)S(1)} %bitcast.32, bf16[2,256,128]{2,1,0:T(8,128)(2,1)S(1)} %collective-permute-done.refs_1_, bf16[2,256,128]{2,1,0:T(8,128)(2,1)S(1)} %collective-permute-done.1.refs_2_, ...), custom_call_target="tpu_custom_call" | custom-call | flops 1073741824 | bytes 6291456 | tf_op jit(solution)/shard_map/pallas_call | solution.py:53
  46.0 16.5 %all_to_all.15 = f32[4,2,256,128]{3,2,1,0:T(8,128)S(1)} all-to-all(f32[4,2,256,128]{3,2,1,0:T(8,128)S(1)} %shard_map.46), channel_id=1, replica_groups=mesh['zq'=2,'zr'=4,'x'=4,'zh'=4,'y'=4,'c'=2] {'x'}, dimensions={0} | all-to-all | bytes 2097152 | tf_op jit(solution)/shard_map/all_to_all | solution.py:94
  62.5 0.0 copy-start.1
  62.5 0.6 abs_reduce_fusion
  64.0 0.2 copy.16
  64.2 0.2 concatenate.3.clone
  64.3 65.3 %all_to_all.16 = f16[32,9,2,128]{3,2,1,0:T(2,128)(2,1)S(1)} all-to-all(f16[32,9,2,128]{3,2,1,0:T(2,128)(2,1)S(1)} %concatenate.3.clone), channel_id=1, replica_groups=mesh['zq'=2,'zr'=4,'x'=4,'zh'=4,'y'=4,'c'=2] {'zh','y','c'}, dimensions={0} | all-to-all | bytes 294912 | tf_op jit(solution)/shard_map/all_to_all | solution.py:107
  129.7 0.0 copy-done.1
  129.7 0.9 convolution_bitcast_fusion
  (5 shorter events, 0.1 us)
Async XLA Ops:
  4.0 4.1 %copy-start = (bf16[2,1,256,128]{3,2,1,0:T(8,128)(2,1)S(1)}, bf16[2,1,256,128]{3,2,1,0:T(8,128)(2,1)}, u32[]{:S(2)}) copy-start(bf16[2,1,256,128]{3,2,1,0:T(8,128)(2,1)} %param.4) | copy-start | bytes 393220
  4.0 39.3 %all-to-all-start = ((bf16[4,2,8,128,128]{4,3,2,1,0:T(8,128)(2,1)}), bf16[4,2,8,128,128]{4,3,2,1,0:T(8,128)(2,1)S(1)}, u32[]{:S(2)}, u32[]{:S(2)}) async-start(bf16[4,2,8,128,128]{4,3,2,1,0:T(8,128)(2,1)} %fusion), calls=%async_computation | async-start | bytes 4194304 | tf_op jit(solution)/shard_map/all_to_all | solution.py:87
  8.1 18.8 %collective-permute-start.3 = (bf16[2,256,128]{2,1,0:T(8,128)(2,1)S(1)}, bf16[2,256,128]{2,1,0:T(8,128)(2,1)S(1)}, u32[]{:S(2)}, u32[]{:S(2)}) collective-permute-start(bf16[2,256,128]{2,1,0:T(8,128)(2,1)S(1)} %bitcast.28), channel_id=1, source_target_pairs={{0,512},{512,0},{1,513},{513,1},{2,514},{514,2},{3,515},{515,3},{4... | collective-permute-start | bytes 393224 | tf_op jit(solution)/shard_map/ppermute | solution.py:83
  17.0 26.4 %collective-permute-start.2 = (bf16[2,256,128]{2,1,0:T(8,128)(2,1)S(1)}, bf16[2,256,128]{2,1,0:T(8,128)(2,1)S(1)}, u32[]{:S(2)}, u32[]{:S(2)}) collective-permute-start(bf16[2,256,128]{2,1,0:T(8,128)(2,1)S(1)} %bitcast.29), channel_id=1, source_target_pairs={{0,384},{128,256},{256,128},{384,0},{1,385},{129,257},{257,129},{3... | collective-permute-start | bytes 393224 | tf_op jit(solution)/shard_map/ppermute | solution.py:90
  20.5 22.8 %collective-permute-start.1 = (bf16[2,256,128]{2,1,0:T(8,128)(2,1)S(1)}, bf16[2,256,128]{2,1,0:T(8,128)(2,1)S(1)}, u32[]{:S(2)}, u32[]{:S(2)}) collective-permute-start(bf16[2,256,128]{2,1,0:T(8,128)(2,1)S(1)} %bitcast.30), channel_id=1, source_target_pairs={{0,256},{128,384},{256,0},{384,128},{1,257},{129,385},{257,1},{385... | collective-permute-start | bytes 393224 | tf_op jit(solution)/shard_map/ppermute | solution.py:90
  23.8 19.5 %collective-permute-start = (bf16[2,256,128]{2,1,0:T(8,128)(2,1)S(1)}, bf16[2,256,128]{2,1,0:T(8,128)(2,1)S(1)}, u32[]{:S(2)}, u32[]{:S(2)}) collective-permute-start(bf16[2,256,128]{2,1,0:T(8,128)(2,1)S(1)} %bitcast.31), channel_id=1, source_target_pairs={{0,128},{128,0},{256,384},{384,256},{1,129},{129,1},{257,385},{385... | collective-permute-start | bytes 393224 | tf_op jit(solution)/shard_map/ppermute | solution.py:90
  62.5 67.2 %copy-start.1 = (f32[2,32,16,1]{1,2,3,0:T(8,128)S(1)}, f32[2,32,16,1]{1,2,3,0:T(8,128)}, u32[]{:S(2)}) copy-start(f32[2,32,16,1]{1,2,3,0:T(8,128)} %constant.34) | copy-start | bytes 12292

commit v4 on v3

--- a/solution.py
+++ b/solution.py
@@ -73,6 +73,52 @@
     )(place, *near, far, op)
 
 
+def mask_kernel(keep_ref, rows_ref, out_ref, taken, masked, load_sems, store_sems):
+    count = rows_ref.shape[1]
+    loads = [
+        pltpu.make_async_copy(rows_ref.at[:, z], taken.at[z], load_sems.at[z])
+        for z in range(count)
+    ]
+    stores = [
+        pltpu.make_async_copy(masked.at[z], out_ref.at[:, :, z], store_sems.at[z])
+        for z in range(count)
+    ]
+    for load in loads:
+        load.start()
+    for z in range(count):
+        loads[z].wait()
+        for x in range(NX):
+            keep = keep_ref[z * NX + x].astype(jnp.float32).astype(jnp.bfloat16)
+            for part in range(2):
+                masked[z, x, part] = taken[z, part, x] * keep
+        stores[z].start()
+    for store in stores:
+        store.wait()
+
+
+def masked_rows(keep, rows):
+    parts, count, _, width, _ = rows.shape
+    return pl.pallas_call(
+        mask_kernel,
+        out_shape=jax.ShapeDtypeStruct((NX, parts, count, width, width), rows.dtype),
+        in_specs=[
+            pl.BlockSpec(memory_space=pltpu.SMEM),
+            pl.BlockSpec(memory_space=pltpu.HBM),
+        ],
+        out_specs=pl.BlockSpec(memory_space=pltpu.HBM),
+        scratch_shapes=[
+            pltpu.VMEM((count, parts, NX, width, width), rows.dtype),
+            pltpu.VMEM((count, NX, parts, width, width), rows.dtype),
+            pltpu.SemaphoreType.DMA((count,)),
+            pltpu.SemaphoreType.DMA((count,)),
+        ],
+        compiler_params=pltpu.CompilerParams(vmem_limit_bytes=60 << 20),
+        cost_estimate=pl.CostEstimate(
+            flops=rows.size, bytes_accessed=4 * rows.size, transcendentals=0
+        ),
+    )(keep, rows)
+
+
 def per_device(shot_rows, surface_op, aperture):
     width = surface_op.shape[3]
     shots = shot_rows.shape[2]
@@ -82,9 +128,8 @@
     own = shot_rows.reshape(2, shots, width)
     crossed = lax.ppermute(own, "zq", [(0, 1), (1, 0)])
 
-    keep = aperture.reshape(ZQ * ZR, NX).astype(jnp.bfloat16)
-    rows = surface_op.reshape(2, ZQ * ZR, NX, width, width) * keep[None, :, :, None, None]
-    op = lax.all_to_all(jnp.transpose(rows, (2, 0, 1, 3, 4)), "x", 0, 0, tiled=True)
+    rows = masked_rows(aperture.reshape(-1), surface_op.reshape(2, ZQ * ZR, NX, width, width))
+    op = lax.all_to_all(rows, "x", 0, 0, tiled=True)
 
     near = [own] + [
         lax.ppermute(own, "zr", [(i, i ^ d) for i in range(ZR)]) for d in range(1, ZR)

time: 131 us -> 130 us (level)
  other arithmetic: 4.6 us -> 0.79 us
  Pallas kernels: 2.67 us -> 5.82 us
    pallas_call x0 -> x1, Pallas kernels: none -> 3.15 us  [masked_rows(): pl.pallas_call(mask_kernel, out_shape=jax.ShapeDtypeStruct((NX, parts, co...]
    transpose x1 -> x0, other arithmetic: 3.13 us -> none  [per_device(): jnp.transpose(rows, (2, 0, 1, 3, 4))]
where the time goes in v4:
time: 130 us
  blocking collectives  98.1 us (75%)
  starting transfers between devices  22.9 us (18%)
  Pallas kernels  5.82 us (4%)
    all_to_all x1, blocking collectives, per_device(): mine = lax.all_to_all(sent, FREQ, 0, 0, tiled=True).astype(jnp.float32)  65.3 us
    all_to_all x1, blocking collectives, per_device(): parts = lax.all_to_all(product(place, near, far, op), 'x', 0, 0, tiled=True)  16.5 us
    all_gather x1, blocking collectives, per_device(): far = lax.all_gather(crossed, 'zr', axis=0)  16.3 us
    ppermute x3, starting transfers between devices, per_device(): lax.ppermute(own, 'zr', [(i, i ^ d) for i in range(ZR)])  9.91 us
    ppermute x1, starting transfers between devices, per_device(): crossed = lax.ppermute(own, 'zq', [(0, 1), (1, 0)])  8.81 us
    all_to_all x1, starting transfers between devices, per_device(): op = lax.all_to_all(rows, 'x', 0, 0, tiled=True)  4.16 us
    pallas_call x1, Pallas kernels, masked_rows(): pl.pallas_call(mask_kernel, out_shape=jax.ShapeDtypeStruct((NX, parts, co...  3.15 us
    pallas_call x1, Pallas kernels, product(): pl.pallas_call(product_kernel, out_shape=jax.ShapeDtypeStruct((NX, 2, sho...  2.67 us
  transfers between devices with their start and end apart: 5, of which 0 were waited for; matrix products, arithmetic and copies ran while one was open for 0% of the time, Pallas kernels for 0%

profile of v4, /device:TPU:33, one launch (start us, length us, event | category | flops | bytes accessed | tf_op | source)
XLA Modules:
  0.0 129.8 jit_solution(4789016457790408882)
XLA Ops:
  0.0 3.2 %shard_map.46 = bf16[4,2,8,128,128]{4,3,2,1,0:T(8,128)(2,1)} custom-call(s32[32]{0:T(128)} %bitcast.35, bf16[2,8,4,128,128]{4,3,2,1,0:T(8,128)(2,1)} %bitcast.32), custom_call_target="tpu_custom_call" | custom-call | flops 1048576 | bytes 4194304 | tf_op jit(solution)/shard_map/pallas_call | solution.py:101
  3.2 0.0 copy-start
  3.2 4.2 %all-to-all-start = ((bf16[4,2,8,128,128]{4,3,2,1,0:T(8,128)(2,1)}), bf16[4,2,8,128,128]{4,3,2,1,0:T(8,128)(2,1)S(1)}, u32[]{:S(2)}, u32[]{:S(2)}) async-start(bf16[4,2,8,128,128]{4,3,2,1,0:T(8,128)(2,1)} %shard_map.46), calls=%async_computation | async-start | bytes 4194304 | tf_op jit(solution)/shard_map/all_to_all | solution.py:132
  7.3 0.0 copy-done
  7.3 8.8 %collective-permute-start.3 = (bf16[2,256,128]{2,1,0:T(8,128)(2,1)S(1)}, bf16[2,256,128]{2,1,0:T(8,128)(2,1)S(1)}, u32[]{:S(2)}, u32[]{:S(2)}) collective-permute-start(bf16[2,256,128]{2,1,0:T(8,128)(2,1)S(1)} %bitcast.27), channel_id=1, source_target_pairs={{0,512},{512,0},{1,513},{513,1},{2,514},{514,2},{3,515},{515,3},{4... | collective-permute-start | bytes 393224 | tf_op jit(solution)/shard_map/ppermute | solution.py:129
  16.1 3.5 %collective-permute-start.2 = (bf16[2,256,128]{2,1,0:T(8,128)(2,1)S(1)}, bf16[2,256,128]{2,1,0:T(8,128)(2,1)S(1)}, u32[]{:S(2)}, u32[]{:S(2)}) collective-permute-start(bf16[2,256,128]{2,1,0:T(8,128)(2,1)S(1)} %bitcast.28), channel_id=1, source_target_pairs={{0,384},{128,256},{256,128},{384,0},{1,385},{129,257},{257,129},{3... | collective-permute-start | bytes 393224 | tf_op jit(solution)/shard_map/ppermute | solution.py:135
  19.7 3.3 %collective-permute-start.1 = (bf16[2,256,128]{2,1,0:T(8,128)(2,1)S(1)}, bf16[2,256,128]{2,1,0:T(8,128)(2,1)S(1)}, u32[]{:S(2)}, u32[]{:S(2)}) collective-permute-start(bf16[2,256,128]{2,1,0:T(8,128)(2,1)S(1)} %bitcast.29), channel_id=1, source_target_pairs={{0,256},{128,384},{256,0},{384,128},{1,257},{129,385},{257,1},{385... | collective-permute-start | bytes 393224 | tf_op jit(solution)/shard_map/ppermute | solution.py:135
  23.0 3.1 %collective-permute-start = (bf16[2,256,128]{2,1,0:T(8,128)(2,1)S(1)}, bf16[2,256,128]{2,1,0:T(8,128)(2,1)S(1)}, u32[]{:S(2)}, u32[]{:S(2)}) collective-permute-start(bf16[2,256,128]{2,1,0:T(8,128)(2,1)S(1)} %bitcast.30), channel_id=1, source_target_pairs={{0,128},{128,0},{256,384},{384,256},{1,129},{129,1},{257,385},{385... | collective-permute-start | bytes 393224 | tf_op jit(solution)/shard_map/ppermute | solution.py:135
  26.1 0.1 pad_add_fusion.place_ref
  26.2 0.0 collective-permute-done.3
  26.2 16.3 %all-gather = bf16[8,256,128]{2,1,0:T(8,128)(2,1)S(1)} all-gather(bf16[2,256,128]{2,1,0:T(8,128)(2,1)S(1)} %collective-permute-done.3), channel_id=2, replica_groups=mesh['zq'=2,'zr'=4,'x'=4,'zh'=4,'y'=4,'c'=2] {'zr'}, dimensions={0}, use_global_device_ids=true | all-gather | bytes 655360 | tf_op jit(solution)/shard_map/all_gather | solution.py:137
  42.5 0.0 collective-permute-done.2.refs_3_
  42.5 0.0 collective-permute-done.1.refs_2_
  42.5 0.0 collective-permute-done.refs_1_
  42.5 0.0 all-to-all-done.refs_5_
  42.5 2.7 %shard_map.47 = f32[4,2,256,128]{3,2,1,0:T(8,128)S(1)} custom-call(s32[2]{0:T(128)S(1)} %pad_add_fusion.place_ref, bf16[2,256,128]{2,1,0:T(8,128)(2,1)S(1)} %bitcast.31, bf16[2,256,128]{2,1,0:T(8,128)(2,1)S(1)} %collective-permute-done.refs_1_, bf16[2,256,128]{2,1,0:T(8,128)(2,1)S(1)} %collective-permute-done.1.refs_2_, ...), custom_call_target="tpu_custom_call" | custom-call | flops 1073741824 | bytes 6291456 | tf_op jit(solution)/shard_map/pallas_call | solution.py:53
  45.2 16.5 %all_to_all.15 = f32[4,2,256,128]{3,2,1,0:T(8,128)S(1)} all-to-all(f32[4,2,256,128]{3,2,1,0:T(8,128)S(1)} %shard_map.47), channel_id=1, replica_groups=mesh['zq'=2,'zr'=4,'x'=4,'zh'=4,'y'=4,'c'=2] {'x'}, dimensions={0} | all-to-all | bytes 2097152 | tf_op jit(solution)/shard_map/all_to_all | solution.py:139
  61.7 0.0 copy-start.1
  61.7 0.6 abs_reduce_fusion
  63.2 0.2 copy.11
  63.4 0.2 concatenate.3.clone
  63.5 65.3 %all_to_all.16 = f16[32,9,2,128]{3,2,1,0:T(2,128)(2,1)S(1)} all-to-all(f16[32,9,2,128]{3,2,1,0:T(2,128)(2,1)S(1)} %concatenate.3.clone), channel_id=1, replica_groups=mesh['zq'=2,'zr'=4,'x'=4,'zh'=4,'y'=4,'c'=2] {'zh','y','c'}, dimensions={0} | all-to-all | bytes 294912 | tf_op jit(solution)/shard_map/all_to_all | solution.py:152
  128.9 0.0 copy-done.1
  128.9 0.9 convolution_bitcast_fusion
  (5 shorter events, 0.1 us)
Async XLA Ops:
  3.2 4.2 %copy-start = (bf16[2,1,256,128]{3,2,1,0:T(8,128)(2,1)S(1)}, bf16[2,1,256,128]{3,2,1,0:T(8,128)(2,1)}, u32[]{:S(2)}) copy-start(bf16[2,1,256,128]{3,2,1,0:T(8,128)(2,1)} %param.4) | copy-start | bytes 393220
  3.2 39.4 %all-to-all-start = ((bf16[4,2,8,128,128]{4,3,2,1,0:T(8,128)(2,1)}), bf16[4,2,8,128,128]{4,3,2,1,0:T(8,128)(2,1)S(1)}, u32[]{:S(2)}, u32[]{:S(2)}) async-start(bf16[4,2,8,128,128]{4,3,2,1,0:T(8,128)(2,1)} %shard_map.46), calls=%async_computation | async-start | bytes 4194304 | tf_op jit(solution)/shard_map/all_to_all | solution.py:132
  7.3 18.8 %collective-permute-start.3 = (bf16[2,256,128]{2,1,0:T(8,128)(2,1)S(1)}, bf16[2,256,128]{2,1,0:T(8,128)(2,1)S(1)}, u32[]{:S(2)}, u32[]{:S(2)}) collective-permute-start(bf16[2,256,128]{2,1,0:T(8,128)(2,1)S(1)} %bitcast.27), channel_id=1, source_target_pairs={{0,512},{512,0},{1,513},{513,1},{2,514},{514,2},{3,515},{515,3},{4... | collective-permute-start | bytes 393224 | tf_op jit(solution)/shard_map/ppermute | solution.py:129
  16.1 26.4 %collective-permute-start.2 = (bf16[2,256,128]{2,1,0:T(8,128)(2,1)S(1)}, bf16[2,256,128]{2,1,0:T(8,128)(2,1)S(1)}, u32[]{:S(2)}, u32[]{:S(2)}) collective-permute-start(bf16[2,256,128]{2,1,0:T(8,128)(2,1)S(1)} %bitcast.28), channel_id=1, source_target_pairs={{0,384},{128,256},{256,128},{384,0},{1,385},{129,257},{257,129},{3... | collective-permute-start | bytes 393224 | tf_op jit(solution)/shard_map/ppermute | solution.py:135
  19.7 22.8 %collective-permute-start.1 = (bf16[2,256,128]{2,1,0:T(8,128)(2,1)S(1)}, bf16[2,256,128]{2,1,0:T(8,128)(2,1)S(1)}, u32[]{:S(2)}, u32[]{:S(2)}) collective-permute-start(bf16[2,256,128]{2,1,0:T(8,128)(2,1)S(1)} %bitcast.29), channel_id=1, source_target_pairs={{0,256},{128,384},{256,0},{384,128},{1,257},{129,385},{257,1},{385... | collective-permute-start | bytes 393224 | tf_op jit(solution)/shard_map/ppermute | solution.py:135
  23.0 19.5 %collective-permute-start = (bf16[2,256,128]{2,1,0:T(8,128)(2,1)S(1)}, bf16[2,256,128]{2,1,0:T(8,128)(2,1)S(1)}, u32[]{:S(2)}, u32[]{:S(2)}) collective-permute-start(bf16[2,256,128]{2,1,0:T(8,128)(2,1)S(1)} %bitcast.30), channel_id=1, source_target_pairs={{0,128},{128,0},{256,384},{384,256},{1,129},{129,1},{257,385},{385... | collective-permute-start | bytes 393224 | tf_op jit(solution)/shard_map/ppermute | solution.py:135
  61.7 67.2 %copy-start.1 = (f32[2,32,16,1]{1,2,3,0:T(8,128)S(1)}, f32[2,32,16,1]{1,2,3,0:T(8,128)}, u32[]{:S(2)}) copy-start(f32[2,32,16,1]{1,2,3,0:T(8,128)} %constant.34) | copy-start | bytes 12292

commit v5 on v4

--- a/solution.py
+++ b/solution.py
@@ -43,16 +43,18 @@
         [jnp.concatenate([op_ref[0, 0, z], op_ref[0, 1, z]], axis=1) for z in order], axis=0
     )
     wide = jnp.dot(rows_ref[...], op, preferred_element_type=jnp.float32)
-    out_ref[0, 0] = wide[:shots, :width] - wide[shots:, width:]
-    out_ref[0, 1] = wide[:shots, width:] + wide[shots:, :width]
+    groups = (-1,) + out_ref.shape[3:]
+    out_ref[0, :, 0] = (wide[:shots, :width] - wide[shots:, width:]).reshape(groups)
+    out_ref[0, :, 1] = (wide[:shots, width:] + wide[shots:, :width]).reshape(groups)
 
 
-def product(place, near, far, op):
+def product(place, near, far, op, total):
     shots, width = far.shape[2:]
+    groups = (total, 2, shots // total, width)
     depth = 2 * ZR * width
     return pl.pallas_call(
         product_kernel,
-        out_shape=jax.ShapeDtypeStruct((NX, 2, shots, width), jnp.float32),
+        out_shape=jax.ShapeDtypeStruct((NX,) + groups, jnp.float32),
         grid_spec=pltpu.PrefetchScalarGridSpec(
             num_scalar_prefetch=1,
             grid=(NX,),
@@ -61,7 +63,7 @@
                 pl.BlockSpec((ZR, 2, shots, width), lambda i, q: (0, 0, 0, 0)),
                 pl.BlockSpec((1, 2, 2 * ZR, width, width), lambda i, q: (i, 0, 0, 0, 0)),
             ],
-            out_specs=pl.BlockSpec((1, 2, shots, width), lambda i, q: (i, 0, 0, 0)),
+            out_specs=pl.BlockSpec((1,) + groups, lambda i, q: (i, 0, 0, 0, 0)),
             scratch_shapes=[pltpu.VMEM((2 * shots, depth), jnp.bfloat16)],
         ),
         compiler_params=pltpu.CompilerParams(vmem_limit_bytes=16 << 20),
@@ -136,12 +138,11 @@
     ]
     far = lax.all_gather(crossed, "zr", axis=0)
 
-    parts = lax.all_to_all(product(place, near, far, op), "x", 0, 0, tiled=True)
+    parts = lax.all_to_all(product(place, near, far, op, total), "x", 0, 0, tiled=True)
     spectra = (parts[0] + parts[1]) + (parts[2] + parts[3])
     peak = jnp.maximum(jnp.max(jnp.abs(spectra)), 2.0**-100)
     level = jnp.floor(jnp.log2(peak))
-    sent = jnp.transpose(spectra.reshape(2, total, shots // total, width), (1, 0, 2, 3))
-    sent = (sent * jnp.exp2(13.0 - level)).astype(jnp.float16)
+    sent = (spectra * jnp.exp2(13.0 - level)).astype(jnp.float16)
     sent = jnp.concatenate(
         [
             sent.reshape(total, shots // total, 2, width),

time: 130 us -> 130 us (level)
  no operation moved by 1% of the time
where the time goes in v5:
time: 130 us
  blocking collectives  98.1 us (75%)
  starting transfers between devices  22.9 us (18%)
  Pallas kernels  5.82 us (4%)
    all_to_all x1, blocking collectives, per_device(): mine = lax.all_to_all(sent, FREQ, 0, 0, tiled=True).astype(jnp.float32)  65.3 us
    all_to_all x1, blocking collectives, per_device(): lax.all_to_all(product(place, near, far, op, total), 'x', 0, 0, tiled=True)  16.5 us
    all_gather x1, blocking collectives, per_device(): far = lax.all_gather(crossed, 'zr', axis=0)  16.3 us
    ppermute x3, starting transfers between devices, per_device(): lax.ppermute(own, 'zr', [(i, i ^ d) for i in range(ZR)])  9.91 us
    ppermute x1, starting transfers between devices, per_device(): crossed = lax.ppermute(own, 'zq', [(0, 1), (1, 0)])  8.81 us
    all_to_all x1, starting transfers between devices, per_device(): op = lax.all_to_all(rows, 'x', 0, 0, tiled=True)  4.16 us
    pallas_call x1, Pallas kernels, masked_rows(): pl.pallas_call(mask_kernel, out_shape=jax.ShapeDtypeStruct((NX, parts, co...  3.15 us
    pallas_call x1, Pallas kernels, product(): pl.pallas_call(product_kernel, out_shape=jax.ShapeDtypeStruct((NX,) + gro...  2.67 us
  transfers between devices with their start and end apart: 5, of which 0 were waited for; matrix products, arithmetic and copies ran while one was open for 0% of the time, Pallas kernels for 0%

profile of v5, /device:TPU:33, one launch (start us, length us, event | category | flops | bytes accessed | tf_op | source)
XLA Modules:
  0.0 129.6 jit_solution(5927948915340948615)
XLA Ops:
  0.0 3.2 %shard_map.46 = bf16[4,2,8,128,128]{4,3,2,1,0:T(8,128)(2,1)} custom-call(s32[32]{0:T(128)} %bitcast.31, bf16[2,8,4,128,128]{4,3,2,1,0:T(8,128)(2,1)} %bitcast.28), custom_call_target="tpu_custom_call" | custom-call | flops 1048576 | bytes 4194304 | tf_op jit(solution)/shard_map/pallas_call | solution.py:103
  3.2 0.0 copy-start
  3.2 4.2 %all-to-all-start = ((bf16[4,2,8,128,128]{4,3,2,1,0:T(8,128)(2,1)}), bf16[4,2,8,128,128]{4,3,2,1,0:T(8,128)(2,1)S(1)}, u32[]{:S(2)}, u32[]{:S(2)}) async-start(bf16[4,2,8,128,128]{4,3,2,1,0:T(8,128)(2,1)} %shard_map.46), calls=%async_computation | async-start | bytes 4194304 | tf_op jit(solution)/shard_map/all_to_all | solution.py:134
  7.3 0.0 copy-done
  7.3 8.8 %collective-permute-start.3 = (bf16[2,256,128]{2,1,0:T(8,128)(2,1)S(1)}, bf16[2,256,128]{2,1,0:T(8,128)(2,1)S(1)}, u32[]{:S(2)}, u32[]{:S(2)}) collective-permute-start(bf16[2,256,128]{2,1,0:T(8,128)(2,1)S(1)} %bitcast.23), channel_id=1, source_target_pairs={{0,512},{512,0},{1,513},{513,1},{2,514},{514,2},{3,515},{515,3},{4... | collective-permute-start | bytes 393224 | tf_op jit(solution)/shard_map/ppermute | solution.py:131
  16.1 3.5 %collective-permute-start.2 = (bf16[2,256,128]{2,1,0:T(8,128)(2,1)S(1)}, bf16[2,256,128]{2,1,0:T(8,128)(2,1)S(1)}, u32[]{:S(2)}, u32[]{:S(2)}) collective-permute-start(bf16[2,256,128]{2,1,0:T(8,128)(2,1)S(1)} %bitcast.24), channel_id=1, source_target_pairs={{0,384},{128,256},{256,128},{384,0},{1,385},{129,257},{257,129},{3... | collective-permute-start | bytes 393224 | tf_op jit(solution)/shard_map/ppermute | solution.py:137
  19.7 3.3 %collective-permute-start.1 = (bf16[2,256,128]{2,1,0:T(8,128)(2,1)S(1)}, bf16[2,256,128]{2,1,0:T(8,128)(2,1)S(1)}, u32[]{:S(2)}, u32[]{:S(2)}) collective-permute-start(bf16[2,256,128]{2,1,0:T(8,128)(2,1)S(1)} %bitcast.25), channel_id=1, source_target_pairs={{0,256},{128,384},{256,0},{384,128},{1,257},{129,385},{257,1},{385... | collective-permute-start | bytes 393224 | tf_op jit(solution)/shard_map/ppermute | solution.py:137
  23.0 3.1 %collective-permute-start = (bf16[2,256,128]{2,1,0:T(8,128)(2,1)S(1)}, bf16[2,256,128]{2,1,0:T(8,128)(2,1)S(1)}, u32[]{:S(2)}, u32[]{:S(2)}) collective-permute-start(bf16[2,256,128]{2,1,0:T(8,128)(2,1)S(1)} %bitcast.26), channel_id=1, source_target_pairs={{0,128},{128,0},{256,384},{384,256},{1,129},{129,1},{257,385},{385... | collective-permute-start | bytes 393224 | tf_op jit(solution)/shard_map/ppermute | solution.py:137
  26.1 0.1 pad_add_fusion.place_ref
  26.2 0.0 collective-permute-done.3
  26.2 16.3 %all-gather = bf16[8,256,128]{2,1,0:T(8,128)(2,1)S(1)} all-gather(bf16[2,256,128]{2,1,0:T(8,128)(2,1)S(1)} %collective-permute-done.3), channel_id=2, replica_groups=mesh['zq'=2,'zr'=4,'x'=4,'zh'=4,'y'=4,'c'=2] {'zr'}, dimensions={0}, use_global_device_ids=true | all-gather | bytes 655360 | tf_op jit(solution)/shard_map/all_gather | solution.py:139
  42.5 0.0 collective-permute-done.2.refs_3_
  42.5 0.0 collective-permute-done.1.refs_2_
  42.5 0.0 collective-permute-done.refs_1_
  42.5 0.0 all-to-all-done.refs_5_
  42.5 2.7 %shard_map.47 = f32[4,32,2,8,128]{4,3,2,1,0:T(8,128)S(1)} custom-call(s32[2]{0:T(128)S(1)} %pad_add_fusion.place_ref, bf16[2,256,128]{2,1,0:T(8,128)(2,1)S(1)} %bitcast.27, bf16[2,256,128]{2,1,0:T(8,128)(2,1)S(1)} %collective-permute-done.refs_1_, bf16[2,256,128]{2,1,0:T(8,128)(2,1)S(1)} %collective-permute-done.1.refs_2_, ...), custom_call_target="tpu_custom_call" | custom-call | flops 1073741824 | bytes 6291456 | tf_op jit(solution)/shard_map/pallas_call | solution.py:55
  45.2 16.5 %all_to_all.15 = f32[4,32,2,8,128]{4,3,2,1,0:T(8,128)S(1)} all-to-all(f32[4,32,2,8,128]{4,3,2,1,0:T(8,128)S(1)} %shard_map.47), channel_id=1, replica_groups=mesh['zq'=2,'zr'=4,'x'=4,'zh'=4,'y'=4,'c'=2] {'x'}, dimensions={0} | all-to-all | bytes 2097152 | tf_op jit(solution)/shard_map/all_to_all | solution.py:141
  61.7 0.0 copy-start.1
  61.7 0.7 abs_reduce_fusion
  63.2 0.2 concatenate.3
  63.3 65.3 %all_to_all.16 = f16[32,9,2,128]{3,2,1,0:T(2,128)(2,1)S(1)} all-to-all(f16[32,9,2,128]{3,2,1,0:T(2,128)(2,1)S(1)} %concatenate.3), channel_id=1, replica_groups=mesh['zq'=2,'zr'=4,'x'=4,'zh'=4,'y'=4,'c'=2] {'zh','y','c'}, dimensions={0} | all-to-all | bytes 294912 | tf_op jit(solution)/shard_map/all_to_all | solution.py:153
  128.7 0.0 copy-done.1
  128.7 0.9 convolution_bitcast_fusion
  (4 shorter events, 0.1 us)
Async XLA Ops:
  3.2 4.2 %copy-start = (bf16[2,1,256,128]{3,2,1,0:T(8,128)(2,1)S(1)}, bf16[2,1,256,128]{3,2,1,0:T(8,128)(2,1)}, u32[]{:S(2)}) copy-start(bf16[2,1,256,128]{3,2,1,0:T(8,128)(2,1)} %param.4) | copy-start | bytes 393220
  3.2 39.4 %all-to-all-start = ((bf16[4,2,8,128,128]{4,3,2,1,0:T(8,128)(2,1)}), bf16[4,2,8,128,128]{4,3,2,1,0:T(8,128)(2,1)S(1)}, u32[]{:S(2)}, u32[]{:S(2)}) async-start(bf16[4,2,8,128,128]{4,3,2,1,0:T(8,128)(2,1)} %shard_map.46), calls=%async_computation | async-start | bytes 4194304 | tf_op jit(solution)/shard_map/all_to_all | solution.py:134
  7.3 18.8 %collective-permute-start.3 = (bf16[2,256,128]{2,1,0:T(8,128)(2,1)S(1)}, bf16[2,256,128]{2,1,0:T(8,128)(2,1)S(1)}, u32[]{:S(2)}, u32[]{:S(2)}) collective-permute-start(bf16[2,256,128]{2,1,0:T(8,128)(2,1)S(1)} %bitcast.23), channel_id=1, source_target_pairs={{0,512},{512,0},{1,513},{513,1},{2,514},{514,2},{3,515},{515,3},{4... | collective-permute-start | bytes 393224 | tf_op jit(solution)/shard_map/ppermute | solution.py:131
  16.1 26.4 %collective-permute-start.2 = (bf16[2,256,128]{2,1,0:T(8,128)(2,1)S(1)}, bf16[2,256,128]{2,1,0:T(8,128)(2,1)S(1)}, u32[]{:S(2)}, u32[]{:S(2)}) collective-permute-start(bf16[2,256,128]{2,1,0:T(8,128)(2,1)S(1)} %bitcast.24), channel_id=1, source_target_pairs={{0,384},{128,256},{256,128},{384,0},{1,385},{129,257},{257,129},{3... | collective-permute-start | bytes 393224 | tf_op jit(solution)/shard_map/ppermute | solution.py:137
  19.7 22.8 %collective-permute-start.1 = (bf16[2,256,128]{2,1,0:T(8,128)(2,1)S(1)}, bf16[2,256,128]{2,1,0:T(8,128)(2,1)S(1)}, u32[]{:S(2)}, u32[]{:S(2)}) collective-permute-start(bf16[2,256,128]{2,1,0:T(8,128)(2,1)S(1)} %bitcast.25), channel_id=1, source_target_pairs={{0,256},{128,384},{256,0},{384,128},{1,257},{129,385},{257,1},{385... | collective-permute-start | bytes 393224 | tf_op jit(solution)/shard_map/ppermute | solution.py:137
  23.0 19.5 %collective-permute-start = (bf16[2,256,128]{2,1,0:T(8,128)(2,1)S(1)}, bf16[2,256,128]{2,1,0:T(8,128)(2,1)S(1)}, u32[]{:S(2)}, u32[]{:S(2)}) collective-permute-start(bf16[2,256,128]{2,1,0:T(8,128)(2,1)S(1)} %bitcast.26), channel_id=1, source_target_pairs={{0,128},{128,0},{256,384},{384,256},{1,129},{129,1},{257,385},{385... | collective-permute-start | bytes 393224 | tf_op jit(solution)/shard_map/ppermute | solution.py:137
  61.7 67.0 %copy-start.1 = (f32[2,32,16,1]{1,2,3,0:T(8,128)S(1)}, f32[2,32,16,1]{1,2,3,0:T(8,128)}, u32[]{:S(2)}) copy-start(f32[2,32,16,1]{1,2,3,0:T(8,128)} %constant.34) | copy-start | bytes 12292
